TPU v7x, 1024 devices: a whole 4x4x32 slice. The times are simulated.
1024 devices in a mesh: dp: 16 (over y_lo, x, core), expert: 64 (over y_hi, z).
Axes of the slice: x: 4, y: 4 (y_hi: 2, y_lo: 2; y = y_hi * 2 + y_lo), z: 32, core: 2. Of those that a mesh axis runs over, the one named last changes fastest.
Arguments:
- grad_out: bfloat16 [8192, 4096], P('expert', 'dp'), may hold values from -6 to 6
- routing: int32 [8192, 6], P('expert'), may hold values from 0 to 63, all different within a row; in each aligned block of 128 rows (0 to 127, 128 to 255, ...) at most 14 rows name the same one
- gates: float32 [8192, 6], P('expert'), may hold values from 0.05 to 1
- scales: float32 [8192], P('expert'), may hold values from 0.25 to 4
- saved_gate: bfloat16 [64, 1408, 896], P('expert'), may hold values from -6 to 6
- saved_up: bfloat16 [64, 1408, 896], P('expert'), may hold values from -6 to 6
- w_gate: bfloat16 [64, 4096, 1408], P('expert', 'dp'), may hold values from -0.09375 to 0.09375
- w_up: bfloat16 [64, 4096, 1408], P('expert', 'dp'), may hold values from -0.09375 to 0.09375
- w_down: bfloat16 [64, 1408, 4096], P('expert', None, 'dp'), may hold values from -0.15625 to 0.15625
Outputs:
- grad_x: bfloat16 [8192, 4096], P('expert', 'dp')
- grad_down: bfloat16 [64, 1408, 4096], P('expert', None, 'dp')
Inputs may be any that keep to these rules, and one draw needn't show every extreme that they name: `routing`: each row names 6 different experts; within each token group of 128 rows no expert is named more than 14 times, a bound that some block reaches.
All inputs are finite; a program needn't handle non-finite values.
Results may differ from a plain program's by a relative error of at most 0.027.
Values may be sent and summed in bfloat16 or wider, within the bound.
A program may use at most 32 MiB of HBM per device.

v0:
```python
import jax
import jax.numpy as jnp
from jax import lax
from jax.sharding import PartitionSpec as P


def activation_grad(hidden_grad, gate_pre, up_pre):
    g = gate_pre.astype(jnp.float32)
    u = up_pre.astype(jnp.float32)
    sig = jax.nn.sigmoid(g)
    dh = hidden_grad.astype(jnp.float32)
    gate_grad = (dh * u * sig * (1.0 + g * (1.0 - sig))).astype(jnp.bfloat16)
    up_grad = (dh * g * sig).astype(jnp.bfloat16)
    return (gate_grad, up_grad)


def contract(left, weights):
    return lax.dot_general(
        left, weights, (((0,), (1,)), ((), ())), preferred_element_type=jnp.float32
    )


def local(grad_out, routing, gates, scales, saved_gate, saved_up, w_gate, w_up, w_down):
    tok_rows, dcols = grad_out.shape
    topk = routing.shape[1]
    groups = lax.axis_size("expert")
    experts = groups * w_gate.shape[0]
    slots = saved_gate.shape[2]
    capacity = slots // groups
    flat_route = routing.reshape(-1)
    hot = (flat_route[:, None] == jnp.arange(experts, dtype=jnp.int32)[None, :]).astype(jnp.int32)
    position = jnp.sum(hot * (jnp.cumsum(hot, axis=0) - 1), axis=1)
    target = flat_route * capacity + position
    select = jnp.arange(experts * capacity, dtype=jnp.int32)[:, None] == target[None, :]
    weight = (gates * scales[:, None]).reshape(-1)
    slot_factor = jnp.sum(jnp.where(select, weight[None, :], 0.0), axis=1)
    collect = jnp.any(select.reshape(experts * capacity, tok_rows, topk), axis=2).astype(
        jnp.bfloat16
    )
    owned_rows = jnp.dot(collect, grad_out, preferred_element_type=jnp.float32)
    sending = (
        (slot_factor[:, None] * owned_rows).astype(jnp.bfloat16).reshape(experts, capacity, dcols)
    )
    arrived = lax.all_to_all(sending, "expert", split_axis=0, concat_axis=0, tiled=True).reshape(
        slots, dcols
    )
    wdown = w_down[0]
    wgate = w_gate[0]
    wup = w_up[0]
    sgate = saved_gate[0]
    sup = saved_up[0]
    partial_value = lax.dot_general(
        wdown, arrived, (((1,), (1,)), ((), ())), preferred_element_type=jnp.float32
    )
    reduced = lax.psum_scatter(
        partial_value.astype(jnp.bfloat16), "dp", scatter_dimension=0, tiled=True
    )
    hidden_grad = lax.all_gather(reduced, "dp", axis=0, tiled=True)
    gate_grad, up_grad = activation_grad(hidden_grad, sgate, sup)
    slot_grad = contract(gate_grad, wgate) + contract(up_grad, wup)
    gate_full = sgate.astype(jnp.float32)
    hidden = (gate_full * jax.nn.sigmoid(gate_full) * sup.astype(jnp.float32)).astype(jnp.bfloat16)
    grad_down = jnp.dot(hidden, arrived, preferred_element_type=jnp.float32).astype(jnp.bfloat16)
    returning = slot_grad.astype(jnp.bfloat16).reshape(groups, capacity, dcols)
    back = lax.all_to_all(returning, "expert", split_axis=0, concat_axis=0, tiled=True).reshape(
        experts * capacity, dcols
    )
    grad_x = lax.dot_general(
        collect, back, (((0,), (0,)), ((), ())), preferred_element_type=jnp.float32
    )
    return (grad_x.astype(jnp.bfloat16), grad_down[None])


def solution(mesh):
    return jax.shard_map(
        local,
        mesh=mesh,
        in_specs=(
            P("expert", "dp"),
            P("expert", None),
            P("expert", None),
            P("expert"),
            P("expert", None, None),
            P("expert", None, None),
            P("expert", "dp", None),
            P("expert", "dp", None),
            P("expert", None, "dp"),
        ),
        out_specs=(P("expert", "dp"), P("expert", None, "dp")),
        check_vma=False,
    )
```

profile of v0, /device:TPU:1, one launch (start us, length us, event | category | flops | bytes accessed | tf_op | source)
XLA Modules:
  0.0 413.6 jit_solution(10766896101459884089)
XLA Ops:
  7.2 0.9 copy.37
  8.4 1.8 reduce-window.6
  10.2 0.3 slice_reduce_fusion
  10.5 0.1 fusion.38
  10.8 0.7 broadcast_multiply_fusion
  11.8 0.7 multiply_add_fusion.1
  12.5 0.4 fusion.17
  12.9 0.4 select_reduce_fusion
  13.3 1.1 fusion.33
  14.6 89.8 %all_to_all.10 = bf16[64,14,256]{2,1,0:T(8,128)(2,1)S(1)} all-to-all(bf16[64,14,256]{2,1,0:T(8,128)(2,1)S(1)} %reshape.63), channel_id=1, replica_groups=mesh['dp'=16,'expert'=64] {'expert'}, dimensions={0} | all-to-all | bytes 917504 | tf_op jit(solution)/shard_map/all_to_all | solution.py:44
  104.5 2.4 fusion.16
  107.0 1.3 dynamic-slice
  108.9 146.9 %all-reduce.3.cloned.1.call-done = bf16[1408,896]{0,1:T(8,128)(2,1)} async-done(((bf16[1408,896]{0,1:T(8,128)(2,1)}), bf16[1408,896]{0,1:T(8,128)(2,1)}) %all-reduce.3.cloned.1.call-update) | async-done | bytes 2523152
  255.8 1.1 constant_dynamic-slice_fusion
  257.0 0.8 copy.42
  257.8 56.1 %all-gather.2.cloned.1.call-done = bf16[1408,896]{1,0:T(8,128)(2,1)} async-done(((bf16[88,896]{1,0:T(8,128)(2,1)}), bf16[1408,896]{1,0:T(8,128)(2,1)}) %all-gather.2.cloned.1.call-update) | async-done | bytes 2523152 | tf_op jit(solution)/shard_map/all_gather | solution.py:58
  314.0 4.2 %fusion.20 = f32[896,256]{1,0:T(8,128)S(1)} fusion(bf16[1,1408,896]{2,1,0:T(8,128)(2,1)} %param.13, bf16[1408,896]{1,0:T(8,128)(2,1)} %all-gather.2.cloned.1.call-done, bf16[1,256,1408]{2,1,0:T(8,128)(2,1)S(1)} %copy-done.4), kind=kOutput, calls=%fused_computation.30 | convolution fusion | flops 656015360 | bytes 6684672 | tf_op jit(solution)/shard_map/dot_general | solution.py:18
  318.2 0.5 copy-done.3
  318.7 2.7 fusion.30
  321.4 0.9 reshape.65
  322.3 25.4 %all-to-all-start.1 = ((bf16[64,14,256]{2,1,0:T(8,128)(2,1)}), bf16[64,14,256]{2,1,0:T(8,128)(2,1)S(1)}, u32[]{:S(2)}, u32[]{:S(2)}) async-start(bf16[64,14,256]{2,1,0:T(8,128)(2,1)} %reshape.65), calls=%async_computation.1 | async-start | bytes 1048576 | tf_op jit(solution)/shard_map/all_to_all | solution.py:65
  347.7 5.1 %fusion.24 = bf16[1,1408,256]{2,1,0:T(8,128)(2,1)} fusion(bf16[896,256]{1,0:T(8,128)(2,1)S(1)} %reshape.64, bf16[1,1408,896]{2,1,0:T(8,128)(2,1)} %param.14, bf16[1,1408,896]{2,1,0:T(8,128)(2,1)} %param.13), kind=kOutput, calls=%fused_computation.32 | convolution fusion | flops 656375808 | bytes 6225920 | tf_op jit(solution)/shard_map/dot_general | solution.py:63
  352.8 52.9 %all-to-all-done.1 = bf16[64,14,256]{2,1,0:T(8,128)(2,1)S(1)} async-done(((bf16[64,14,256]{2,1,0:T(8,128)(2,1)}), bf16[64,14,256]{2,1,0:T(8,128)(2,1)S(1)}, u32[]{:S(2)}, u32[]{:S(2)}) %all-to-all-start.1) | async-done | bytes 458784 | tf_op jit(solution)/shard_map/all_to_all | solution.py:65
  405.8 1.0 convolution_convert_fusion.2
  (27 shorter events, 1.3 us)
Async XLA Ops:
  7.2 97.3 %copy-start = (bf16[1,1408,256]{2,1,0:T(8,128)(2,1)S(1)}, bf16[1,1408,256]{2,1,0:T(8,128)(2,1)}, u32[]{:S(2)}) copy-start(bf16[1,1408,256]{2,1,0:T(8,128)(2,1)} %param.17) | copy-start | bytes 2162692
  7.2 248.7 %all-reduce.3.cloned.1.call-start = ((), (), s32[]{:S(2)}) async-start(), calls=%async_computation.3 | async-start | bytes 5046272
  106.9 207.1 %copy-start.4 = (bf16[1,256,1408]{2,1,0:T(8,128)(2,1)S(1)}, bf16[1,256,1408]{2,1,0:T(8,128)(2,1)}, u32[]{:S(2)}) copy-start(bf16[1,256,1408]{2,1,0:T(8,128)(2,1)} %param.16) | copy-start | bytes 2162692
  106.9 207.0 %all-gather.2.cloned.1.call-start = ((), (), s32[]{:S(2)}) async-start(), calls=%async_computation.2 | async-start | bytes 2680832 | tf_op jit(solution)/shard_map/all_gather | solution.py:58
  257.8 60.4 %copy-start.5 = (bf16[1,256,1408]{2,1,0:T(8,128)(2,1)S(1)}, bf16[1,256,1408]{2,1,0:T(8,128)(2,1)}, u32[]{:S(2)}) copy-start(bf16[1,256,1408]{2,1,0:T(8,128)(2,1)} %param.15) | copy-start | bytes 2162692
  313.9 4.3 %copy-start.1 = (bf16[1,1408,896]{2,1,0:T(8,128)(2,1)S(1)}, bf16[1,1408,896]{2,1,0:T(8,128)(2,1)}, u32[]{:S(2)}) copy-start(bf16[1,1408,896]{2,1,0:T(8,128)(2,1)} %param.13) | copy-start | bytes 7569412
  313.9 4.3 %copy-start.2 = (bf16[1,1408,896]{2,1,0:T(8,128)(2,1)S(1)}, bf16[1,1408,896]{2,1,0:T(8,128)(2,1)}, u32[]{:S(2)}) copy-start(bf16[1,1408,896]{2,1,0:T(8,128)(2,1)} %param.14) | copy-start | bytes 7569412
  313.9 4.7 %copy-start.3 = (bf16[1408,896]{1,0:T(8,128)(2,1)S(1)}, bf16[1408,896]{1,0:T(8,128)(2,1)}, u32[]{:S(2)}) copy-start(bf16[1408,896]{1,0:T(8,128)(2,1)} %all-gather.2.cloned.1.call-done) | copy-start | bytes 7569412
  322.3 83.4 %all-to-all-start.1 = ((bf16[64,14,256]{2,1,0:T(8,128)(2,1)}), bf16[64,14,256]{2,1,0:T(8,128)(2,1)S(1)}, u32[]{:S(2)}, u32[]{:S(2)}) async-start(bf16[64,14,256]{2,1,0:T(8,128)(2,1)} %reshape.65), calls=%async_computation.1 | async-start | bytes 1048576 | tf_op jit(solution)/shard_map/all_to_all | solution.py:65
Sparse Core Ops, SparseCore 0:
  107.0 148.7 all-reduce.2
  259.2 54.7 all-gather.1
where the time goes:
time: 417 us; the launch traced here: 414 us
  waiting for transfers between devices  256 us (61%)
  blocking collectives  89.8 us (22%)
  starting transfers between devices  25.4 us (6%)
  matrix products  16.5 us (4%)
  between operations  14.9 us (4%)
  local copies, waits for them, and re-layouts  6.92 us (2%)
  other arithmetic  4.19 us (1%)
    unnamed x3, waiting for transfers between devices  147 us
    all_to_all x1, blocking collectives, local(): lax.all_to_all(sending, 'expert', split_axis=0, concat_axis=0, tiled=True)  89.8 us
    all_gather x1, waiting for transfers between devices, local(): hidden_grad = lax.all_gather(reduced, 'dp', axis=0, tiled=True)  56.1 us
    all_to_all x1, waiting for transfers between devices, local(): lax.all_to_all(returning, 'expert', split_axis=0, concat_axis=0, tiled=True)  52.9 us
    all_to_all x1, starting transfers between devices, local(): lax.all_to_all(returning, 'expert', split_axis=0, concat_axis=0, tiled=True)  25.4 us
  transfers between devices with their start and end apart: 3, of which 3 were waited for; matrix products, arithmetic and copies ran while one was open for 2% of the time, Pallas kernels for 0%

commit v1 on v0

v1 whole, which is shorter than its diff:
```python
import functools

import jax
import jax.numpy as jnp
from jax import lax
from jax.experimental import pallas as pl
from jax.experimental.pallas import tpu as pltpu
from jax.sharding import PartitionSpec as P

MESH = pl.DeviceIdType.MESH
PAD = 16
F32 = jnp.float32
BF16 = jnp.bfloat16


def nt(a, b):
    return lax.dot_general(a, b, (((1,), (1,)), ((), ())), preferred_element_type=F32)


def nn(a, b):
    return lax.dot_general(a, b, (((1,), (0,)), ((), ())), preferred_element_type=F32)


def iota(shape, dim):
    return lax.broadcasted_iota(jnp.int32, shape, dim)


def onehot(cond):
    return jnp.where(cond, 1.0, 0.0).astype(BF16)


def kernel(
    nz,
    cap,
    go_ref,
    rt_ref,
    gt_ref,
    sc_ref,
    sg_hbm,
    su_hbm,
    wg_hbm,
    wu_hbm,
    wd_hbm,
    gx_ref,
    gd_hbm,
    send,
    arr,
    sib,
    back,
    part,
    rsin,
    hid,
    fac_g,
    fac_u,
    sgv,
    suv,
    hact,
    wg,
    wu,
    wd,
    ret,
    gdv,
    coll_t,
    a_send,
    a_recv,
    b_send,
    b_recv,
    r_send,
    r_recv,
    g_send,
    g_recv,
    w_send,
    w_recv,
    s_send,
    s_recv,
    l_sem,
):
    tok, dcols = go_ref.shape
    topk = rt_ref.shape[1]
    ff, slots = sgv.shape
    ne = 2 * nz
    nq = part.shape[1]
    rows = part.shape[2]
    half = nq * rows
    dp = lax.axis_index("dp")
    e = lax.axis_index("expert")
    c = lax.rem(dp, 2)
    base = dp - c
    q = lax.div(dp, 2)
    yh = lax.div(e, nz)
    z = lax.rem(e, nz)
    h = lax.rem(z, 2)
    zz = lax.div(z, 2)

    barrier = pltpu.get_barrier_semaphore()

    def greet(i, carry):
        idx = lax.rem(e * 2 + c + i, 2 * ne)
        pl.semaphore_signal(
            barrier,
            inc=1,
            device_id=(base + lax.rem(idx, 2), lax.div(idx, 2)),
            device_id_type=MESH,
        )
        return carry

    lax.fori_loop(1, 2 * ne, greet, 0)
    for i in range(1, nq):
        pl.semaphore_signal(
            barrier,
            inc=1,
            device_id=(lax.rem(q + i, nq) * 2 + c, e),
            device_id_type=MESH,
        )

    loads = [
        pltpu.make_async_copy(sg_hbm.at[0], sgv, l_sem.at[0]),
        pltpu.make_async_copy(su_hbm.at[0], suv, l_sem.at[1]),
        pltpu.make_async_copy(wd_hbm.at[0], wd.at[c], l_sem.at[2]),
        pltpu.make_async_copy(wg_hbm.at[0], wg.at[c], l_sem.at[3]),
        pltpu.make_async_copy(wu_hbm.at[0], wu.at[c], l_sem.at[4]),
    ]
    for copy in loads:
        copy.start()

    lane_e = iota((tok, ne), 1)
    named = jnp.zeros((tok, ne), F32)
    gate = jnp.zeros((tok, ne), F32)
    for k in range(topk):
        hit = rt_ref[:, k : k + 1] == lane_e
        named = named + jnp.where(hit, 1.0, 0.0)
        gate = gate + jnp.where(hit, gt_ref[:, k : k + 1], 0.0)
    earlier = onehot(iota((tok, tok), 0) > iota((tok, tok), 1))
    position = nn(earlier, named.astype(BF16))
    value = (named * (position + 1.0)).astype(BF16)
    spread = (iota((ne * PAD, ne), 0) // PAD) == iota((ne * PAD, ne), 1)
    wanted = ((iota((ne * PAD, tok), 0) % PAD) + 1).astype(F32)
    pick = nt(onehot(spread), value) == wanted
    gates_at = lax.dot_general(
        jnp.where(spread, 1.0, 0.0),
        gate,
        (((1,), (1,)), ((), ())),
        precision=lax.Precision.HIGHEST,
        preferred_element_type=F32,
    )
    slot_factor = jnp.sum(
        jnp.where(pick, gates_at * sc_ref[...], 0.0), axis=1, keepdims=True
    )
    owned = nn(onehot(pick), go_ref[...])
    send[...] = (slot_factor * owned).astype(BF16)
    spread_t = iota((ne, ne * PAD), 0) == (iota((ne, ne * PAD), 1) // PAD)
    wanted_t = ((iota((tok, ne * PAD), 1) % PAD) + 1).astype(F32)
    coll_t[...] = onehot(nn(value, onehot(spread_t)) == wanted_t)

    pl.semaphore_wait(barrier, 2 * ne - 1 + nq - 1)

    other = base + 1 - c
    weights = []
    for k in range(2):
        yt = yh + k - 2 * yh * k

        def scatter(i, carry, k=k, yt=yt):
            j = nz - 1 - i
            step = lax.div(j + 1, 2) * (2 * lax.rem(j, 2) - 1)
            to = yt * nz + lax.rem(z + step + nz, nz)
            source = send.at[pl.ds(pl.multiple_of(to * PAD, PAD), PAD)]
            target = arr.at[k, c, pl.ds(pl.multiple_of(zz * PAD, PAD), PAD)]
            remote = pltpu.make_async_remote_copy(
                src_ref=source,
                dst_ref=target,
                send_sem=a_send.at[k],
                recv_sem=a_recv.at[k],
                device_id=(base + h, to),
                device_id_type=MESH,
            )
            if k == 0:
                mine = jnp.logical_and(to == e, h == c)

                @pl.when(mine)
                def _():
                    pltpu.make_async_copy(source, target, a_recv.at[k]).start()

                @pl.when(jnp.logical_not(mine))
                def _():
                    remote.start()
            else:
                remote.start()
            return carry

        lax.fori_loop(0, nz, scatter, 0)
        if k == 0:
            for n, (src, dst) in enumerate(((wd_hbm, wd), (wg_hbm, wg), (wu_hbm, wu))):
                copy = pltpu.make_async_remote_copy(
                    src_ref=src.at[0],
                    dst_ref=dst.at[c],
                    send_sem=w_send.at[n],
                    recv_sem=w_recv.at[n],
                    device_id=(other, e),
                    device_id_type=MESH,
                )
                copy.start()
                weights.append(copy)

    loads[0].wait()
    loads[1].wait()

    def slot_of(index, core):
        k = index // half
        g = (yh + k - 2 * yh * k) * nz + ((index % half) // PAD) * 2 + core
        place = index % PAD
        return jnp.where(place < cap, g * cap + place, -1)

    take = onehot(slot_of(iota((2 * half, slots), 0), c) == iota((2 * half, slots), 1))
    tile = 128

    def factors(i, carry):
        f0 = pl.multiple_of(i * tile, tile)
        g = nt(take, sgv[pl.ds(f0, tile), :])
        u = nt(take, suv[pl.ds(f0, tile), :])
        sig = jax.nn.sigmoid(g)
        fac_g[:, pl.ds(f0, tile)] = u * sig * (1.0 + g * (1.0 - sig))
        fac_u[:, pl.ds(f0, tile)] = g * sig
        return carry

    lax.fori_loop(0, ff // tile, factors, 0)

    def activate(i, carry):
        f0 = pl.multiple_of(i * 32, 32)
        g = sgv[pl.ds(f0, 32), :].astype(F32)
        u = suv[pl.ds(f0, 32), :].astype(F32)
        hact[pl.ds(f0, 32), :] = (g * jax.nn.sigmoid(g) * u).astype(BF16)
        return carry

    lax.fori_loop(0, ff // 32, activate, 0)

    for copy in loads[2:]:
        copy.wait()

    sibs = []
    for k in range(2):
        pltpu.make_async_copy(arr.at[k], arr.at[k], a_recv.at[k]).wait()
        if k == 0:
            weights[0].wait_recv()
        copy = pltpu.make_async_remote_copy(
            src_ref=arr.at[k, 1 - c],
            dst_ref=sib.at[pl.ds(k * half, half)],
            send_sem=s_send.at[k],
            recv_sem=s_recv.at[k],
            device_id=(other, e),
            device_id_type=MESH,
        )
        copy.start()
        sibs.append(copy)

        def partial_sums(i, carry, k=k):
            f0 = pl.multiple_of(i * tile, tile)
            value = nt(arr[k, 0], wd[0, pl.ds(f0, tile), :]) + nt(
                arr[k, 1], wd[1, pl.ds(f0, tile), :]
            )
            part[k, :, :, pl.ds(f0, tile)] = value.astype(BF16).reshape(nq, rows, tile)
            return carry

        lax.fori_loop(0, ff // tile, partial_sums, 0)

        def exchange(i, carry, k=k):
            to = lax.rem(q + i, nq)
            pltpu.make_async_remote_copy(
                src_ref=part.at[k, to],
                dst_ref=rsin.at[k, q],
                send_sem=r_send.at[k],
                recv_sem=r_recv.at[k],
                device_id=(to * 2 + c, e),
                device_id_type=MESH,
            ).start()
            return carry

        lax.fori_loop(1, nq, exchange, 0)
        rsin[k, q] = part[k, q]
        everyone = pl.ds(0, nq - 1)
        pltpu.make_async_copy(
            rsin.at[k, everyone], rsin.at[k, everyone], r_recv.at[k]
        ).wait()
        total = rsin[k, 0].astype(F32)
        for i in range(1, nq):
            total = total + rsin[k, i].astype(F32)
        hid[k, q] = total.astype(BF16)

        def share(i, carry, k=k):
            to = lax.rem(q + i, nq)
            pltpu.make_async_remote_copy(
                src_ref=hid.at[k, q],
                dst_ref=hid.at[k, q],
                send_sem=g_send.at[k],
                recv_sem=g_recv.at[k],
                device_id=(to * 2 + c, e),
                device_id_type=MESH,
            ).start()
            return carry

        lax.fori_loop(1, nq, share, 0)
        if k == 0:
            weights[1].wait_recv()
            weights[2].wait_recv()
        pltpu.make_async_copy(
            hid.at[k, everyone], hid.at[k, everyone], g_recv.at[k]
        ).wait()

        dh = hid[k].astype(F32).reshape(half, ff)
        gate_grad = (dh * fac_g[pl.ds(k * half, half), :]).astype(BF16)
        up_grad = (dh * fac_u[pl.ds(k * half, half), :]).astype(BF16)
        for n in range(2):
            ret[k, n] = (nt(gate_grad, wg[n]) + nt(up_grad, wu[n])).astype(BF16)

        yt = yh + k - 2 * yh * k

        def give_back(i, carry, k=k, yt=yt):
            j = nz // 2 - 1 - i
            step = lax.div(j + 1, 2) * (2 * lax.rem(j, 2) - 1)
            zt = lax.rem(zz + step + nz // 2, nz // 2)
            to = yt * nz + zt * 2 + c
            target = back.at[pl.ds(pl.multiple_of(e * PAD, PAD), PAD)]
            for n in range(2):
                source = ret.at[k, n, pl.ds(pl.multiple_of(zt * PAD, PAD), PAD)]
                remote = pltpu.make_async_remote_copy(
                    src_ref=source,
                    dst_ref=target,
                    send_sem=b_send,
                    recv_sem=b_recv,
                    device_id=(base + n, to),
                    device_id_type=MESH,
                )
                if k == 0:
                    mine = jnp.logical_and(to == e, c == n)

                    @pl.when(mine)
                    def _(source=source):
                        pltpu.make_async_copy(source, target, b_recv).start()

                    @pl.when(jnp.logical_not(mine))
                    def _(remote=remote):
                        remote.start()
                else:
                    remote.start()
            return carry

        lax.fori_loop(0, nz // 2, give_back, 0)

    sibs[0].wait_recv()
    sibs[1].wait_recv()
    own = jnp.concatenate([arr[0, c], arr[1, c]], axis=0)
    order = iota((slots, 2 * half), 1)
    slot = iota((slots, 2 * half), 0)
    natural = (
        nn(onehot(slot_of(order, c) == slot), own)
        + nn(onehot(slot_of(order, 1 - c) == slot), sib[...])
    ).astype(BF16)

    def down(i, carry):
        f0 = pl.multiple_of(i * tile, tile)
        gdv[pl.ds(f0, tile), :] = nn(hact[pl.ds(f0, tile), :], natural).astype(BF16)
        return carry

    lax.fori_loop(0, ff // tile, down, 0)
    out = pltpu.make_async_copy(gdv, gd_hbm.at[0], l_sem.at[0])
    out.start()

    pltpu.make_async_copy(back, back, b_recv).wait()
    gx_ref[...] = nn(coll_t[...], back[...]).astype(BF16)

    out.wait()
    for copy in weights + sibs:
        copy.wait_send()
    for k in range(2):
        pltpu.make_async_copy(
            rsin.at[k, pl.ds(0, nq - 1)], rsin.at[k, pl.ds(0, nq - 1)], r_send.at[k]
        ).wait()
        pltpu.make_async_copy(
            rsin.at[k, pl.ds(0, nq - 1)], rsin.at[k, pl.ds(0, nq - 1)], g_send.at[k]
        ).wait()
    less = (nz - 1) * PAD
    full = nz * PAD
    pltpu.make_async_copy(
        send.at[pl.ds(0, full)], send.at[pl.ds(0, full)], a_send.at[1]
    ).wait()

    @pl.when(h == c)
    def _():
        pltpu.make_async_copy(
            send.at[pl.ds(0, less)], send.at[pl.ds(0, less)], a_send.at[0]
        ).wait()
        pltpu.make_async_copy(
            send.at[pl.ds(0, full + less)], send.at[pl.ds(0, full + less)], b_send
        ).wait()

    @pl.when(h != c)
    def _():
        pltpu.make_async_copy(
            send.at[pl.ds(0, full)], send.at[pl.ds(0, full)], a_send.at[0]
        ).wait()
        pltpu.make_async_copy(send, send, b_send).wait()


def local(grad_out, routing, gates, scales, saved_gate, saved_up, w_gate, w_up, w_down):
    tok, dcols = grad_out.shape
    ne = lax.axis_size("expert")
    nq = lax.axis_size("dp") // 2
    nz = ne // 2
    _, ff, slots = saved_gate.shape
    cap = slots // ne
    half = nz // 2 * PAD
    rows = half // nq
    vmem = pl.BlockSpec(memory_space=pltpu.VMEM)
    hbm = pl.BlockSpec(memory_space=pl.ANY)
    dma = pltpu.SemaphoreType.DMA
    return pl.pallas_call(
        functools.partial(kernel, nz, cap),
        out_shape=(
            jax.ShapeDtypeStruct((tok, dcols), BF16),
            jax.ShapeDtypeStruct((1, ff, dcols), BF16),
        ),
        in_specs=[vmem] * 4 + [hbm] * 5,
        out_specs=(vmem, hbm),
        scratch_shapes=[
            pltpu.VMEM((ne * PAD, dcols), BF16),
            pltpu.VMEM((2, 2, half, dcols), BF16),
            pltpu.VMEM((2 * half, dcols), BF16),
            pltpu.VMEM((ne * PAD, dcols), BF16),
            pltpu.VMEM((2, nq, rows, ff), BF16),
            pltpu.VMEM((2, nq, rows, ff), BF16),
            pltpu.VMEM((2, nq, rows, ff), BF16),
            pltpu.VMEM((2 * half, ff), F32),
            pltpu.VMEM((2 * half, ff), F32),
            pltpu.VMEM((ff, slots), BF16),
            pltpu.VMEM((ff, slots), BF16),
            pltpu.VMEM((ff, slots), BF16),
            pltpu.VMEM((2, dcols, ff), BF16),
            pltpu.VMEM((2, dcols, ff), BF16),
            pltpu.VMEM((2, ff, dcols), BF16),
            pltpu.VMEM((2, 2, half, dcols), BF16),
            pltpu.VMEM((ff, dcols), BF16),
            pltpu.VMEM((tok, ne * PAD), BF16),
            dma((2,)),
            dma((2,)),
            dma,
            dma,
            dma((2,)),
            dma((2,)),
            dma((2,)),
            dma((2,)),
            dma((3,)),
            dma((3,)),
            dma((2,)),
            dma((2,)),
            dma((5,)),
        ],
        compiler_params=pltpu.CompilerParams(
            collective_id=0, has_side_effects=True, vmem_limit_bytes=56 * 1024 * 1024
        ),
    )(
        grad_out,
        routing,
        gates,
        scales.reshape(1, tok),
        saved_gate,
        saved_up,
        w_gate,
        w_up,
        w_down,
    )


def solution(mesh):
    return jax.shard_map(
        local,
        mesh=mesh,
        in_specs=(
            P("expert", "dp"),
            P("expert", None),
            P("expert", None),
            P("expert"),
            P("expert", None, None),
            P("expert", None, None),
            P("expert", "dp", None),
            P("expert", "dp", None),
            P("expert", None, "dp"),
        ),
        out_specs=(P("expert", "dp"), P("expert", None, "dp")),
        check_vma=False,
    )
```

time: 417 us -> 147 us (0.35)
  waiting for transfers between devices: 256 us -> 0 us
  Pallas kernels: 0 us -> 139 us
  blocking collectives: 89.8 us -> 0 us
  starting transfers between devices: 25.4 us -> 0 us
  matrix products: 16.5 us -> 0 us
  between operations: 14.9 us -> 0.64 us
  other arithmetic: 4.19 us -> 0 us
    unnamed x3 -> x0, waiting for transfers between devices: 147 us -> none
    pallas_call x0 -> x1, Pallas kernels: none -> 139 us  [local(): pl.pallas_call(functools.partial(kernel, nz, cap), out_shape=(jax.ShapeDt...]
    all_to_all x1 -> x0, blocking collectives: 89.8 us -> none  [local(): lax.all_to_all(sending, 'expert', split_axis=0, concat_axis=0, tiled=True)]
    all_gather x1 -> x0, waiting for transfers between devices: 56.1 us -> none  [local(): hidden_grad = lax.all_gather(reduced, 'dp', axis=0, tiled=True)]
    all_to_all x1 -> x0, waiting for transfers between devices: 52.9 us -> none  [local(): lax.all_to_all(returning, 'expert', split_axis=0, concat_axis=0, tiled=True)]
    all_to_all x1 -> x0, starting transfers between devices: 25.4 us -> none  [local(): lax.all_to_all(returning, 'expert', split_axis=0, concat_axis=0, tiled=True)]
    dot_general x6 -> x0, matrix products: 16.5 us -> none  [the longest x2 6.92 us: contract(): lax.dot_general(left, weights, (((0,), (1,)), ((), ())), preferred_elemen...]
  transfers between devices with their start and end apart: 3 -> 0, of which waited for: 3 -> 0; matrix products, arithmetic and copies ran while one was open for 2% -> 0% of each run, Pallas kernels for 0% -> 0%
where the time goes in v1:
time: 147 us; the launch traced here: 146 us
  Pallas kernels  139 us (95%)
  local copies, waits for them, and re-layouts  6.33 us (4%)
    pallas_call x1, Pallas kernels, local(): pl.pallas_call(functools.partial(kernel, nz, cap), out_shape=(jax.ShapeDt...  139 us
    unnamed x4, local copies, waits for them, and re-layouts  6.33 us

profile of v1, /device:TPU:1, one launch (start us, length us, event | category | flops | bytes accessed | tf_op | source)
XLA Modules:
  0.0 146.4 jit_solution(3433769348668554357)
XLA Ops:
  0.6 1.4 copy.11.rt_ref
  2.1 1.4 copy.12.gt_ref
  3.5 139.4 %shard_map.104 = (bf16[128,256]{1,0:T(8,128)(2,1)}, bf16[1,1408,256]{2,1,0:T(8,128)(2,1)}) custom-call(bf16[128,256]{1,0:T(8,128)(2,1)} %go_ref.1, s32[128,6]{1,0:T(8,128)} %copy.11.rt_ref, f32[128,6]{1,0:T(8,128)} %copy.12.gt_ref, f32[1,128]{1,0:T(1,128)} %bitcast.1, bf16[1,1408,896]{2,1,0:T(8,128)(2,1)} %sg_hbm.1, bf16[1,1408,896]{2,1,0:T(8,128)(2,1)} %su_hbm.1, ...), custom_call_target="tpu_custom_call" | custom-call | tf_op jit(solution)/shard_map/pallas_call | solution.py:415
  142.9 1.5 %copy.15 = bf16[128,256]{1,0:T(8,128)(2,1)} copy(bf16[128,256]{1,0:T(8,128)(2,1)} %get-tuple-element.4) | data formatting | bytes 131072
  144.4 2.0 %copy.16 = bf16[1,1408,256]{2,1,0:T(8,128)(2,1)} copy(bf16[1,1408,256]{2,1,0:T(8,128)(2,1)} %get-tuple-element.5) | data formatting | bytes 1441792

commit v2 on v1

v2 whole, which is shorter than its diff:
```python
import functools

import jax
import jax.numpy as jnp
from jax import lax
from jax.experimental import pallas as pl
from jax.experimental.pallas import tpu as pltpu
from jax.sharding import PartitionSpec as P

MESH = pl.DeviceIdType.MESH
PAD = 16
PARTS = 4
F32 = jnp.float32
BF16 = jnp.bfloat16


def nt(a, b):
    return lax.dot_general(a, b, (((1,), (1,)), ((), ())), preferred_element_type=F32)


def nn(a, b):
    return lax.dot_general(a, b, (((1,), (0,)), ((), ())), preferred_element_type=F32)


def iota(shape, dim):
    return lax.broadcasted_iota(jnp.int32, shape, dim)


def onehot(cond):
    return jnp.where(cond, 1.0, 0.0).astype(BF16)


def kernel(
    nz,
    cap,
    go_ref,
    rt_ref,
    gt_ref,
    sc_ref,
    sg_hbm,
    su_hbm,
    wg_hbm,
    wu_hbm,
    wd_hbm,
    gx_ref,
    gd_hbm,
    send,
    arr,
    sib,
    back,
    part,
    rsin,
    hid,
    fac_g,
    fac_u,
    sgv,
    suv,
    hact,
    wg,
    wu,
    wd,
    ret,
    gdv,
    coll_t,
    a_send,
    a_recv,
    b_send,
    b_recv,
    r_send,
    r_recv,
    g_send,
    g_recv,
    w_send,
    w_recv,
    s_send,
    s_recv,
    l_sem,
):
    tok, dcols = go_ref.shape
    topk = rt_ref.shape[0]
    ff, slots = sgv.shape
    ne = 2 * nz
    chunks, nq, rows, _ = part.shape
    size = nq * rows
    turns = size // (2 * PAD)
    dp = lax.axis_index("dp")
    e = lax.axis_index("expert")
    c = lax.rem(dp, 2)
    base = dp - c
    q = lax.div(dp, 2)
    yh = lax.div(e, nz)
    z = lax.rem(e, nz)
    h = lax.rem(z, 2)

    def hop(t, odd):
        far = nz // 2 - odd - 2 * ((t + 1 - odd) // 2)
        return far * (2 * ((t + odd) % 2) - 1)

    barrier = pltpu.get_barrier_semaphore()

    def greet(i, carry):
        step = lax.div(i + 1, 2) * (2 * lax.rem(i, 2) - 1)
        zt = lax.rem(z + nz // 2 + step + nz, nz)
        for yt in range(2):
            there = yt * nz + zt

            @pl.when(jnp.logical_or(there != e, h != c))
            def _(there=there):
                pl.semaphore_signal(
                    barrier, inc=1, device_id=(base + h, there), device_id_type=MESH
                )

            @pl.when(
                jnp.logical_and(
                    lax.rem(zt, 2) == c, jnp.logical_or(there != e, h == c)
                )
            )
            def _(there=there):
                pl.semaphore_signal(
                    barrier, inc=1, device_id=(base + 1 - h, there), device_id_type=MESH
                )

        return carry

    lax.fori_loop(0, nz, greet, 0)
    for i in range(1, nq):
        pl.semaphore_signal(
            barrier,
            inc=1,
            device_id=(lax.rem(q + i, nq) * 2 + c, e),
            device_id_type=MESH,
        )

    loads = [
        pltpu.make_async_copy(sg_hbm.at[0], sgv, l_sem.at[0]),
        pltpu.make_async_copy(su_hbm.at[0], suv, l_sem.at[1]),
        pltpu.make_async_copy(wd_hbm.at[0], wd.at[c], l_sem.at[2]),
        pltpu.make_async_copy(wg_hbm.at[0], wg.at[c], l_sem.at[3]),
        pltpu.make_async_copy(wu_hbm.at[0], wu.at[c], l_sem.at[4]),
    ]
    for copy in loads:
        copy.start()

    row_e = iota((ne, tok), 0)
    named = jnp.zeros((ne, tok), F32)
    gate = jnp.zeros((ne, tok), F32)
    for k in range(topk):
        hit = rt_ref[k : k + 1, :] == row_e
        named = named + jnp.where(hit, 1.0, 0.0)
        gate = gate + jnp.where(hit, gt_ref[k : k + 1, :], 0.0)
    earlier = onehot(iota((tok, tok), 0) < iota((tok, tok), 1))
    value = named * (nn(named.astype(BF16), earlier) + 1.0)
    spread = (iota((ne * PAD, ne), 0) // PAD) == iota((ne * PAD, ne), 1)
    wanted = ((iota((ne * PAD, tok), 0) % PAD) + 1).astype(F32)
    pick = nn(onehot(spread), value.astype(BF16)) == wanted
    gates_at = lax.dot_general(
        jnp.where(spread, 1.0, 0.0),
        gate,
        (((1,), (0,)), ((), ())),
        precision=lax.Precision.HIGHEST,
        preferred_element_type=F32,
    )
    slot_factor = jnp.sum(
        jnp.where(pick, gates_at * sc_ref[...], 0.0), axis=1, keepdims=True
    )
    owned = nn(onehot(pick), go_ref[...])
    send[...] = (slot_factor * owned).astype(BF16)

    pl.semaphore_wait(barrier, ne + ne // 2 + nq - 1 - jnp.where(h == c, 1, 0))

    other = base + 1 - c

    def scatter(i, carry, n, last):
        k = lax.rem(i, 2)
        odd = lax.rem(lax.div(i, 2), 2)
        turn = lax.div(i, 4)
        step = hop(n * turns + turn, odd)
        to = (yh + k - 2 * yh * k) * nz + lax.rem(z - step + nz, nz)
        source = send.at[pl.ds(pl.multiple_of(to * PAD, PAD), PAD)]
        place = pl.multiple_of((turn * 2 + k) * PAD, PAD)
        target = arr.at[n, c, pl.ds(place, PAD)]
        remote = pltpu.make_async_remote_copy(
            src_ref=source,
            dst_ref=target,
            send_sem=a_send.at[n],
            recv_sem=a_recv.at[n],
            device_id=(base + h, to),
            device_id_type=MESH,
        )
        if last:
            mine = jnp.logical_and(to == e, h == c)

            @pl.when(mine)
            def _():
                pltpu.make_async_copy(source, target, a_recv.at[n]).start()

            @pl.when(jnp.logical_not(mine))
            def _():
                remote.start()
        else:
            remote.start()
        return carry

    def issue(n):
        last = n == chunks - 1
        lax.fori_loop(0, 4 * turns, functools.partial(scatter, n=n, last=last), 0)

    def left(n):
        out = pl.ds(0, 4 * turns * PAD)
        pltpu.make_async_copy(send.at[out], send.at[out], a_send.at[n]).wait()

    issue(0)
    weights = []
    for n, (src, dst) in enumerate(((wd_hbm, wd), (wg_hbm, wg), (wu_hbm, wu))):
        copy = pltpu.make_async_remote_copy(
            src_ref=src.at[0],
            dst_ref=dst.at[c],
            send_sem=w_send.at[n],
            recv_sem=w_recv.at[n],
            device_id=(other, e),
            device_id_type=MESH,
        )
        copy.start()
        weights.append(copy)

    spread_t = iota((ne, ne * PAD), 0) == (iota((ne, ne * PAD), 1) // PAD)
    wanted_t = ((iota((tok, ne * PAD), 1) % PAD) + 1).astype(F32)
    coll_t[...] = onehot(nn(value.T.astype(BF16), onehot(spread_t)) == wanted_t)

    loads[0].wait()
    loads[1].wait()

    def slot_of(index, core):
        k = (index // PAD) % 2
        odd = lax.rem(z + core, 2)
        zt = (z + hop(index // (2 * PAD), odd) + nz) % nz
        g = (yh + k - 2 * yh * k) * nz + zt
        place = index % PAD
        return jnp.where(place < cap, g * cap + place, -1)

    total = chunks * size
    take = onehot(slot_of(iota((total, 1), 0), c) == iota((total, slots), 1))
    tile = 128

    def factors(i, carry):
        f0 = pl.multiple_of(i * tile, tile)
        g = nt(take, sgv[pl.ds(f0, tile), :])
        u = nt(take, suv[pl.ds(f0, tile), :])
        sig = jax.nn.sigmoid(g)
        fac_g[:, pl.ds(f0, tile)] = u * sig * (1.0 + g * (1.0 - sig))
        fac_u[:, pl.ds(f0, tile)] = g * sig
        return carry

    lax.fori_loop(0, ff // tile, factors, 0)
    issue(1)

    def activate(i, carry):
        f0 = pl.multiple_of(i * 32, 32)
        g = sgv[pl.ds(f0, 32), :].astype(F32)
        u = suv[pl.ds(f0, 32), :].astype(F32)
        hact[pl.ds(f0, 32), :] = (g * jax.nn.sigmoid(g) * u).astype(BF16)
        return carry

    lax.fori_loop(0, ff // 32, activate, 0)

    for copy in loads[2:]:
        copy.wait()

    sibs = []
    everyone = pl.ds(0, nq - 1)

    def reduce_start(n):
        pltpu.make_async_copy(arr.at[n], arr.at[n], a_recv.at[n]).wait()
        if n == 0:
            weights[0].wait_recv()

        def partial_sums(i, carry):
            f0 = pl.multiple_of(i * tile, tile)
            value = nt(arr[n, 0], wd[0, pl.ds(f0, tile), :]) + nt(
                arr[n, 1], wd[1, pl.ds(f0, tile), :]
            )
            part[n, :, :, pl.ds(f0, tile)] = value.astype(BF16).reshape(nq, rows, tile)
            return carry

        lax.fori_loop(0, ff // tile, partial_sums, 0)

        def exchange(i, carry):
            to = lax.rem(q + i, nq)
            pltpu.make_async_remote_copy(
                src_ref=part.at[n, to],
                dst_ref=rsin.at[n, q],
                send_sem=r_send.at[n],
                recv_sem=r_recv.at[n],
                device_id=(to * 2 + c, e),
                device_id_type=MESH,
            ).start()
            return carry

        lax.fori_loop(1, nq, exchange, 0)
        copy = pltpu.make_async_remote_copy(
            src_ref=arr.at[n, 1 - c],
            dst_ref=sib.at[pl.ds(n * size, size)],
            send_sem=s_send.at[n],
            recv_sem=s_recv.at[n],
            device_id=(other, e),
            device_id_type=MESH,
        )
        copy.start()
        sibs.append(copy)
        rsin[n, q] = part[n, q]

    def gather_start(n):
        pltpu.make_async_copy(
            rsin.at[n, everyone], rsin.at[n, everyone], r_recv.at[n]
        ).wait()
        value = rsin[n, 0].astype(F32)
        for i in range(1, nq):
            value = value + rsin[n, i].astype(F32)
        hid[n, q] = value.astype(BF16)

        def share(i, carry):
            to = lax.rem(q + i, nq)
            pltpu.make_async_remote_copy(
                src_ref=hid.at[n, q],
                dst_ref=hid.at[n, q],
                send_sem=g_send.at[n],
                recv_sem=g_recv.at[n],
                device_id=(to * 2 + c, e),
                device_id_type=MESH,
            ).start()
            return carry

        lax.fori_loop(1, nq, share, 0)

    def return_start(n):
        if n == 0:
            weights[1].wait_recv()
            weights[2].wait_recv()
        pltpu.make_async_copy(
            hid.at[n, everyone], hid.at[n, everyone], g_recv.at[n]
        ).wait()
        dh = hid[n].astype(F32).reshape(size, ff)
        gate_grad = (dh * fac_g[pl.ds(n * size, size), :]).astype(BF16)
        up_grad = (dh * fac_u[pl.ds(n * size, size), :]).astype(BF16)
        for m in range(2):
            ret[n, m] = (nt(gate_grad, wg[m]) + nt(up_grad, wu[m])).astype(BF16)

        def give_back(i, carry):
            k = lax.rem(i, 2)
            turn = lax.div(i, 2)
            step = hop(n * turns + turn, lax.rem(z + c, 2))
            to = (yh + k - 2 * yh * k) * nz + lax.rem(z + step + nz, nz)
            target = back.at[pl.ds(pl.multiple_of(e * PAD, PAD), PAD)]
            for m in range(2):
                source = ret.at[n, m, pl.ds(pl.multiple_of(i * PAD, PAD), PAD)]
                remote = pltpu.make_async_remote_copy(
                    src_ref=source,
                    dst_ref=target,
                    send_sem=b_send,
                    recv_sem=b_recv,
                    device_id=(base + m, to),
                    device_id_type=MESH,
                )
                if n == chunks - 1:
                    mine = jnp.logical_and(to == e, c == m)

                    @pl.when(mine)
                    def _(source=source):
                        pltpu.make_async_copy(source, target, b_recv).start()

                    @pl.when(jnp.logical_not(mine))
                    def _(remote=remote):
                        remote.start()
                else:
                    remote.start()
            return carry

        lax.fori_loop(0, 2 * turns, give_back, 0)

    issue(2)
    reduce_start(0)
    gather_start(0)
    issue(3)
    return_start(0)
    reduce_start(1)
    gather_start(1)
    reduce_start(2)
    return_start(1)
    gather_start(2)
    reduce_start(3)
    return_start(2)
    gather_start(3)
    return_start(3)
    left(0)
    left(1)
    left(2)
    for copy in sibs:
        copy.wait_recv()
    own = jnp.concatenate([arr[n, c] for n in range(chunks)], axis=0)
    order = iota((1, total), 1)
    slot = iota((slots, total), 0)
    natural = (
        nn(onehot(slot_of(order, c) == slot), own)
        + nn(onehot(slot_of(order, 1 - c) == slot), sib[...])
    ).astype(BF16)

    def down(i, carry):
        f0 = pl.multiple_of(i * tile, tile)
        gdv[pl.ds(f0, tile), :] = nn(hact[pl.ds(f0, tile), :], natural).astype(BF16)
        return carry

    lax.fori_loop(0, ff // tile, down, 0)
    out = pltpu.make_async_copy(gdv, gd_hbm.at[0], l_sem.at[0])
    out.start()

    pltpu.make_async_copy(back, back, b_recv).wait()
    gx_ref[...] = nn(coll_t[...], back[...]).astype(BF16)

    out.wait()
    for copy in weights + sibs:
        copy.wait_send()
    for n in range(chunks):
        for sem in (r_send, g_send):
            pltpu.make_async_copy(
                rsin.at[n, everyone], rsin.at[n, everyone], sem.at[n]
            ).wait()
    ends = pl.ds(0, (4 * turns - 1) * PAD)
    less = pl.ds(0, (ne - 1) * PAD)

    @pl.when(h == c)
    def _():
        pltpu.make_async_copy(send.at[ends], send.at[ends], a_send.at[chunks - 1]).wait()
        pltpu.make_async_copy(send.at[less], send.at[less], b_send).wait()

    @pl.when(h != c)
    def _():
        left(chunks - 1)
        pltpu.make_async_copy(send, send, b_send).wait()


def finish(x_ref, d_ref, gx_ref, gd_ref, x_mem, d_mem, sem_in, sem_out):
    size = d_ref.shape[1] // PARTS
    blocks = [(x_ref, x_mem, gx_ref)]
    for i in range(PARTS):
        block = pl.ds(i * size, size)
        blocks.append((d_ref.at[:, block], d_mem.at[:, block], gd_ref.at[:, block]))
    fetches, writes = [], []
    for i, (src, mem, dst) in enumerate(blocks):
        fetches.append(pltpu.make_async_copy(src, mem, sem_in.at[i]))
        writes.append(pltpu.make_async_copy(mem, dst, sem_out.at[i]))
        fetches[i].start()
    for fetch, write in zip(fetches, writes):
        fetch.wait()
        write.start()
    for write in writes:
        write.wait()


def local(grad_out, routing, gates, scales, saved_gate, saved_up, w_gate, w_up, w_down):
    tok, dcols = grad_out.shape
    ne = lax.axis_size("expert")
    nq = lax.axis_size("dp") // 2
    nz = ne // 2
    _, ff, slots = saved_gate.shape
    cap = slots // ne
    chunks = min(4, nz // 2)
    size = nz * PAD // chunks
    rows = size // nq
    total = chunks * size
    vmem = pl.BlockSpec(memory_space=pltpu.VMEM)
    hbm = pl.BlockSpec(memory_space=pl.ANY)
    dma = pltpu.SemaphoreType.DMA
    tmp_x, tmp_d = pl.pallas_call(
        functools.partial(kernel, nz, cap),
        out_shape=(
            jax.ShapeDtypeStruct((tok, dcols), BF16),
            jax.ShapeDtypeStruct((1, ff, dcols), BF16),
        ),
        in_specs=[vmem] * 4 + [hbm] * 5,
        out_specs=(vmem, hbm),
        scratch_shapes=[
            pltpu.VMEM((ne * PAD, dcols), BF16),
            pltpu.VMEM((chunks, 2, size, dcols), BF16),
            pltpu.VMEM((total, dcols), BF16),
            pltpu.VMEM((ne * PAD, dcols), BF16),
            pltpu.VMEM((chunks, nq, rows, ff), BF16),
            pltpu.VMEM((chunks, nq, rows, ff), BF16),
            pltpu.VMEM((chunks, nq, rows, ff), BF16),
            pltpu.VMEM((total, ff), F32),
            pltpu.VMEM((total, ff), F32),
            pltpu.VMEM((ff, slots), BF16),
            pltpu.VMEM((ff, slots), BF16),
            pltpu.VMEM((ff, slots), BF16),
            pltpu.VMEM((2, dcols, ff), BF16),
            pltpu.VMEM((2, dcols, ff), BF16),
            pltpu.VMEM((2, ff, dcols), BF16),
            pltpu.VMEM((chunks, 2, size, dcols), BF16),
            pltpu.VMEM((ff, dcols), BF16),
            pltpu.VMEM((tok, ne * PAD), BF16),
            dma((chunks,)),
            dma((chunks,)),
            dma,
            dma,
            dma((chunks,)),
            dma((chunks,)),
            dma((chunks,)),
            dma((chunks,)),
            dma((3,)),
            dma((3,)),
            dma((chunks,)),
            dma((chunks,)),
            dma((5,)),
        ],
        compiler_params=pltpu.CompilerParams(
            collective_id=0, has_side_effects=True, vmem_limit_bytes=56 * 1024 * 1024
        ),
    )(
        grad_out,
        routing.T,
        gates.T,
        scales.reshape(1, tok),
        saved_gate,
        saved_up,
        w_gate,
        w_up,
        w_down,
    )
    return pl.pallas_call(
        finish,
        out_shape=(
            jax.ShapeDtypeStruct((tok, dcols), BF16),
            jax.ShapeDtypeStruct((1, ff, dcols), BF16),
        ),
        in_specs=[hbm, hbm],
        out_specs=(hbm, hbm),
        scratch_shapes=[
            pltpu.VMEM((tok, dcols), BF16),
            pltpu.VMEM((1, ff, dcols), BF16),
            dma((PARTS + 1,)),
            dma((PARTS + 1,)),
        ],
    )(tmp_x, tmp_d)


def solution(mesh):
    return jax.shard_map(
        local,
        mesh=mesh,
        in_specs=(
            P("expert", "dp"),
            P("expert", None),
            P("expert", None),
            P("expert"),
            P("expert", None, None),
            P("expert", None, None),
            P("expert", "dp", None),
            P("expert", "dp", None),
            P("expert", None, "dp"),
        ),
        out_specs=(P("expert", "dp"), P("expert", None, "dp")),
        check_vma=False,
    )
```

time: 147 us -> 133 us (0.905)
  Pallas kernels: 139 us -> 132 us
  local copies, waits for them, and re-layouts: 6.33 us -> 0 us
    pallas_call x1, Pallas kernels: 139 us -> 130 us  [local(): pl.pallas_call(functools.partial(kernel, nz, cap), out_shape=(jax.ShapeDt...]
    unnamed x4 -> x0, local copies, waits for them, and re-layouts: 6.33 us -> none
    pallas_call x0 -> x1, Pallas kernels: none -> 1.98 us  [local(): pl.pallas_call(finish, out_shape=(jax.ShapeDtypeStruct((tok, dcols), BF16...]
where the time goes in v2:
time: 133 us; the launch traced here: 132 us
  Pallas kernels  132 us (99%)
    pallas_call x1, Pallas kernels, local(): pl.pallas_call(functools.partial(kernel, nz, cap), out_shape=(jax.ShapeDt...  130 us

profile of v2, /device:TPU:1, one launch (start us, length us, event | category | flops | bytes accessed | tf_op | source)
XLA Modules:
  0.0 132.4 jit_solution(17315260855210047312)
XLA Ops:
  0.6 129.8 %shard_map.104 = (bf16[128,256]{1,0:T(8,128)(2,1)}, bf16[1,1408,256]{2,1,0:T(8,128)(2,1)}) custom-call(bf16[128,256]{1,0:T(8,128)(2,1)} %go_ref.1, s32[6,128]{1,0:T(8,128)} %bitcast.3, f32[6,128]{1,0:T(8,128)} %bitcast.4, f32[1,128]{1,0:T(1,128)} %bitcast.5, bf16[1,1408,896]{2,1,0:T(8,128)(2,1)} %sg_hbm.1, bf16[1,1408,896]{2,1,0:T(8,128)(2,1)} %su_hbm.1, ...), custom_call_target="tpu_custom_call" | custom-call | tf_op jit(solution)/shard_map/pallas_call | solution.py:473
  130.4 2.0 %shard_map.105 = (bf16[128,256]{1,0:T(8,128)(2,1)}, bf16[1,1408,256]{2,1,0:T(8,128)(2,1)}) custom-call(bf16[128,256]{1,0:T(8,128)(2,1)} %get-tuple-element.4.x_ref, bf16[1,1408,256]{2,1,0:T(8,128)(2,1)} %get-tuple-element.5.d_ref), custom_call_target="tpu_custom_call" | custom-call | tf_op jit(solution)/shard_map/pallas_call | solution.py:528

commit v3 on v2

--- a/solution.py
+++ b/solution.py
@@ -268,6 +268,7 @@
 
     sibs = []
     everyone = pl.ds(0, nq - 1)
+    partners = sorted(range(1, nq), key=lambda i: i % 4 != 2)
 
     def reduce_start(n):
         pltpu.make_async_copy(arr.at[n], arr.at[n], a_recv.at[n]).wait()
@@ -284,7 +285,7 @@
 
         lax.fori_loop(0, ff // tile, partial_sums, 0)
 
-        def exchange(i, carry):
+        for i in partners:
             to = lax.rem(q + i, nq)
             pltpu.make_async_remote_copy(
                 src_ref=part.at[n, to],
@@ -294,9 +295,6 @@
                 device_id=(to * 2 + c, e),
                 device_id_type=MESH,
             ).start()
-            return carry
-
-        lax.fori_loop(1, nq, exchange, 0)
         copy = pltpu.make_async_remote_copy(
             src_ref=arr.at[n, 1 - c],
             dst_ref=sib.at[pl.ds(n * size, size)],
@@ -318,7 +316,7 @@
             value = value + rsin[n, i].astype(F32)
         hid[n, q] = value.astype(BF16)
 
-        def share(i, carry):
+        for i in partners:
             to = lax.rem(q + i, nq)
             pltpu.make_async_remote_copy(
                 src_ref=hid.at[n, q],
@@ -328,9 +326,6 @@
                 device_id=(to * 2 + c, e),
                 device_id_type=MESH,
             ).start()
-            return carry
-
-        lax.fori_loop(1, nq, share, 0)
 
     def return_start(n):
         if n == 0:
@@ -378,9 +373,9 @@
         lax.fori_loop(0, 2 * turns, give_back, 0)
 
     issue(2)
+    issue(3)
     reduce_start(0)
     gather_start(0)
-    issue(3)
     return_start(0)
     reduce_start(1)
     gather_start(1)

time: 133 us -> 133 us (level)
  no operation moved by 1% of the time
where the time goes in v3:
time: 133 us
  Pallas kernels  132 us (99%)
    pallas_call x1, Pallas kernels, local(): pl.pallas_call(functools.partial(kernel, nz, cap), out_shape=(jax.ShapeDt...  130 us

profile of v3, /device:TPU:1, one launch (start us, length us, event | category | flops | bytes accessed | tf_op | source)
XLA Modules:
  0.0 132.6 jit_solution(5498527442790398258)
XLA Ops:
  0.6 130.0 %shard_map.104 = (bf16[128,256]{1,0:T(8,128)(2,1)}, bf16[1,1408,256]{2,1,0:T(8,128)(2,1)}) custom-call(bf16[128,256]{1,0:T(8,128)(2,1)} %go_ref.1, s32[6,128]{1,0:T(8,128)} %bitcast.3, f32[6,128]{1,0:T(8,128)} %bitcast.4, f32[1,128]{1,0:T(1,128)} %bitcast.5, bf16[1,1408,896]{2,1,0:T(8,128)(2,1)} %sg_hbm.1, bf16[1,1408,896]{2,1,0:T(8,128)(2,1)} %su_hbm.1, ...), custom_call_target="tpu_custom_call" | custom-call | tf_op jit(solution)/shard_map/pallas_call | solution.py:468
  130.7 2.0 %shard_map.105 = (bf16[128,256]{1,0:T(8,128)(2,1)}, bf16[1,1408,256]{2,1,0:T(8,128)(2,1)}) custom-call(bf16[128,256]{1,0:T(8,128)(2,1)} %get-tuple-element.4.x_ref, bf16[1,1408,256]{2,1,0:T(8,128)(2,1)} %get-tuple-element.5.d_ref), custom_call_target="tpu_custom_call" | custom-call | tf_op jit(solution)/shard_map/pallas_call | solution.py:523
